TPU v7x, 128 devices: a whole 4x4x4 slice. The times are simulated.
128 devices in a mesh: walk: 16 (over x, z), pan: 8 (over y, core).
Axes of the slice: x: 4, y: 4, z: 4, core: 2. Of those that a mesh axis runs over, the one named last changes fastest.
Arguments:
- dlog: bfloat16 [32768, 4096], P('walk', 'pan'), may hold values from 0 to 2
- dener: bfloat16 [32768, 4096], P('walk', 'pan'), may hold values from -0.5 to 2.5
- energy: float32 [32768], P('walk'), may hold values from -3 to -1
- mask: int32 [16], replicated, may hold values 0 or 1
- owner: int32 [16], replicated, may hold values from 0 to 15, each once
Outputs:
- correlation: float32 [4096, 4096], P('walk', 'pan')
- hamilton: float32 [4096, 4096], P('walk', 'pan')
Inputs may be any that keep to these rules, and one draw needn't show every extreme that they name: `owner`: each block number appears once.
All inputs are finite; a program needn't handle non-finite values.
Results may differ from a plain program's by a relative error of at most 0.005.
Values may be sent and summed in bfloat16 or wider, within the bound.
A program may use at most 128 MiB of HBM per device.

v0:
```python
import jax
import jax.numpy as jnp
from jax import lax
from jax.sharding import PartitionSpec as P

BLOCK = 256


def per_device(dlog, dener, energy, mask, owner):
    wdev, width = dlog.shape
    total = wdev * lax.axis_size("walk")
    full = width * lax.axis_size("pan")
    nblocks = full // BLOCK
    first = lax.axis_index("pan") * (width // BLOCK)
    local_mask = lax.dynamic_slice_in_dim(mask, first, width // BLOCK)
    colmask = jnp.repeat(local_mask, BLOCK).astype(jnp.float32)
    om = dlog.astype(jnp.float32) * colmask
    gm = dener.astype(jnp.float32) * colmask
    osum, gsum, esum = lax.psum((jnp.sum(om, 0), jnp.sum(gm, 0), jnp.sum(energy)), "walk")
    ocf = om - osum / total
    oc = ocf.astype(jnp.bfloat16)
    hc = ((energy - esum / total)[:, None] * ocf + gm - gsum / total).astype(jnp.bfloat16)
    gathered = lax.all_gather(oc, "pan", axis=1, tiled=True)
    ordered = jnp.take(gathered.reshape(wdev, nblocks, BLOCK), owner, axis=1).reshape(wdev, full)
    right_side = jnp.concatenate([oc, hc], 1)
    dims = (((0,), (0,)), ((), ()))
    terms = lax.dot_general(ordered, right_side, dims, preferred_element_type=jnp.float32)
    shares = lax.psum_scatter(terms, "walk", scatter_dimension=0, tiled=True)
    shares = shares / total
    return (shares[:, :width], shares[:, width:])


def solution(mesh):
    return jax.shard_map(
        per_device,
        mesh=mesh,
        in_specs=(P("walk", "pan"), P("walk", "pan"), P("walk"), P(), P()),
        out_specs=(P("walk", "pan"), P("walk", "pan")),
        check_vma=False,
    )
```

profile of v0, /device:TPU:1, one launch (start us, length us, event | category | flops | bytes accessed | tf_op | source)
XLA Modules:
  0.0 329.0 jit_solution(5466082891426086491)
XLA Ops:
  7.2 0.0 copy-start.3
  7.2 0.0 copy-start
  7.2 0.0 all-gather.2.cloned.1.call-start
  7.2 0.9 dynamic-slice_convert_fusion
  8.1 0.1 broadcast_bitcast_fusion
  8.2 1.3 reduce_sum.28
  9.5 3.1 fusion.4
  12.6 36.5 %all-reduce = (f32[512]{0:T(512)S(1)}, f32[512]{0:T(512)S(1)}, f32[]{:T(128)}) all-reduce(f32[512]{0:T(512)S(1)} %get-tuple-element.3, f32[512]{0:T(512)S(1)} %get-tuple-element.2, f32[]{:T(128)} %reduce_sum.28), channel_id=1, replica_groups=mesh['walk'=16,'pan'=8] {'walk'}, use_global_device_ids=true, to_apply=%region_1.0 | all-reduce | flops 1025 | bytes 8200 | tf_op jit(solution)/shard_map/psum | solution.py:19
  49.7 0.0 copy-done.3
  49.7 0.0 copy-done
  49.7 0.0 copy-start.4
  49.8 3.9 %subtract_convert_fusion = (bf16[2048,512]{1,0:T(8,128)(2,1)}, bf16[2048,512]{1,0:T(8,128)(2,1)}) fusion(bf16[2048,512]{1,0:T(8,128)(2,1)S(1)} %copy-done, bf16[2048,512]{1,0:T(8,128)(2,1)} %param.5, f32[512]{0:T(512)S(1)} %get-tuple-element.11, f32[2048]{0:T(1024)S(1)} %broadcast_subtract_fusion, f32[512]{0:T(512)S(1)} %get-tuple-element.12, f32[512]{0:T(512)S(1)} %bitcast.11), kind=kLoop, calls=%fused_computation.6 | loop fusion | flops 10485760 | bytes 8402944 | tf_op jit(solution)/shard_map/convert_element_type | solution.py:22
  53.6 0.0 all-gather.2.cloned.1.call-update
  53.7 0.0 reduce-scatter.2.cloned.1.call-start
  53.7 0.0 copy-done.4
  53.7 0.1 broadcast_in_dim.24
  53.9 89.0 %all-gather.2.cloned.1.call-done = bf16[2048,4096]{1,0:T(8,128)(2,1)} async-done(((bf16[2048,512]{1,0:T(8,128)(2,1)}), bf16[2048,4096]{1,0:T(8,128)(2,1)}) %all-gather.2.cloned.1.call-update) | async-done | bytes 16777232 | tf_op jit(solution)/shard_map/all_gather | solution.py:23
  142.8 22.6 %copy.7 = bf16[2048,4096]{0,1:T(8,128)(2,1)} copy(bf16[2048,4096]{1,0:T(8,128)(2,1)} %all-gather.2.cloned.1.call-done) | data formatting | bytes 33554432 | tf_op jit(solution)/shard_map/all_gather | solution.py:23
  165.4 13.0 %gather_fusion = bf16[16,2048,256]{1,2,0:T(8,128)(2,1)} fusion(bf16[2048,16,256]{0,2,1:T(8,128)(2,1)} %bitcast.9, s32[1024]{0:T(1024)S(1)} %pad_clamp_fusion), kind=kCustom, calls=%fused_computation | custom fusion | bytes 33554496 | tf_op jit(solution)/shard_map/jit(_take)/gather | solution.py:24
  178.4 0.0 copy-start.1
  178.4 0.0 copy-start.2
  178.4 9.5 %bitcast_select_fusion = bf16[2048,4096]{0,1:T(8,128)(2,1)S(1)} fusion(bf16[16,2048,256]{1,2,0:T(8,128)(2,1)} %gather_fusion, pred[4096]{0:T(1024)(128)(4,1)S(1)} %broadcast_in_dim.25), kind=kLoop, calls=%fused_computation.1 | loop fusion | flops 8388608 | bytes 33558528 | tf_op jit(solution)/shard_map/jit(_take)/select_n | solution.py:24
  188.0 0.0 copy-done.1
  188.0 0.0 copy-done.2
  188.0 20.8 %fusion = f32[4096,1024]{1,0:T(8,128)} fusion(bf16[2048,4096]{0,1:T(8,128)(2,1)S(1)} %bitcast_select_fusion, bf16[2048,512]{1,0:T(8,128)(2,1)S(1)} %copy-done.2, bf16[2048,512]{1,0:T(8,128)(2,1)S(1)} %copy-done.1), kind=kOutput, calls=%fused_computation.2 | convolution fusion | flops 17188257792 | bytes 37748736 | tf_op jit(solution)/shard_map/dot_general | solution.py:27
  208.8 0.0 reduce-scatter.2.cloned.1.call-update
  208.8 111.0 %reduce-scatter.2.cloned.1.call-done = f32[256,1024]{1,0:T(8,128)} async-done(((f32[4096,1024]{1,0:T(8,128)}), f32[256,1024]{1,0:T(8,128)}) %reduce-scatter.2.cloned.1.call-update) | async-done | bytes 1048592 | tf_op jit(solution)/shard_map/reduce_scatter | solution.py:28
  319.8 1.3 broadcast_multiply_fusion
  321.1 1.0 fusion.9
  (7 shorter events, 0.0 us)
Async XLA Ops:
  7.2 42.5 %copy-start.3 = (f32[2048]{0:T(1024)S(1)}, f32[2048]{0:T(1024)}, u32[]{:S(2)}) copy-start(f32[2048]{0:T(1024)} %param.7) | copy-start | bytes 24580
  7.2 42.6 %copy-start = (bf16[2048,512]{1,0:T(8,128)(2,1)S(1)}, bf16[2048,512]{1,0:T(8,128)(2,1)}, u32[]{:S(2)}) copy-start(bf16[2048,512]{1,0:T(8,128)(2,1)} %param.6) | copy-start | bytes 6291460
  7.2 135.6 %all-gather.2.cloned.1.call-start = ((), (), s32[]{:S(2)}) async-start(), calls=%async_computation.1 | async-start | bytes 18874368 | tf_op jit(solution)/shard_map/all_gather | solution.py:23
  49.7 4.0 %copy-start.4 = (s32[16]{0:T(128)S(1)}, s32[16]{0:T(128)}, u32[]{:S(2)}) copy-start(s32[16]{0:T(128)} %param.9) | copy-start | bytes 196
  53.7 266.1 %reduce-scatter.2.cloned.1.call-start = ((), (), s32[]{:S(2)}) async-start(), calls=%async_computation.2 | async-start | bytes 17825792 | tf_op jit(solution)/shard_map/reduce_scatter | solution.py:28
  178.4 9.6 %copy-start.1 = (bf16[2048,512]{1,0:T(8,128)(2,1)S(1)}, bf16[2048,512]{1,0:T(8,128)(2,1)}, u32[]{:S(2)}) copy-start(bf16[2048,512]{1,0:T(8,128)(2,1)} %get-tuple-element.8) | copy-start | bytes 6291460
  178.4 9.6 %copy-start.2 = (bf16[2048,512]{1,0:T(8,128)(2,1)S(1)}, bf16[2048,512]{1,0:T(8,128)(2,1)}, u32[]{:S(2)}) copy-start(bf16[2048,512]{1,0:T(8,128)(2,1)} %get-tuple-element.7) | copy-start | bytes 6291460
Sparse Core Ops, SparseCore 0:
  53.8 88.9 all-gather.1
  209.0 110.7 reduce-scatter.1
where the time goes:
time: 330 us; the launch traced here: 329 us
  waiting for transfers between devices  200 us (61%)
  local copies, waits for them, and re-layouts  36.8 us (11%)
  blocking collectives  36.5 us (11%)
  matrix products  20.8 us (6%)
  other arithmetic  20.1 us (6%)
  between operations  14.8 us (4%)
    reduce_scatter x1, waiting for transfers between devices, per_device(): shares = lax.psum_scatter(terms, 'walk', scatter_dimension=0, tiled=True)  111 us
    all_gather x1, waiting for transfers between devices, per_device(): gathered = lax.all_gather(oc, 'pan', axis=1, tiled=True)  89 us
    psum x1, blocking collectives, per_device(): lax.psum((jnp.sum(om, 0), jnp.sum(gm, 0), jnp.sum(energy)), 'walk')  36.5 us
    all_gather x1, local copies, waits for them, and re-layouts, per_device(): gathered = lax.all_gather(oc, 'pan', axis=1, tiled=True)  22.6 us
    dot_general x1, matrix products, per_device(): lax.dot_general(ordered, right_side, dims, preferred_element_type=jnp.flo...  20.8 us
    gather x1, local copies, waits for them, and re-layouts, per_device(): jnp.take(gathered.reshape(wdev, nblocks, BLOCK), owner, axis=1)  13 us
    select_n x2, other arithmetic, per_device(): jnp.take(gathered.reshape(wdev, nblocks, BLOCK), owner, axis=1)  9.55 us
  transfers between devices with their start and end apart: 2, of which 2 were waited for; matrix products, arithmetic and copies ran while one was open for 0% of the time, Pallas kernels for 0%

commit v1 on v0

--- a/solution.py
+++ b/solution.py
@@ -7,6 +7,16 @@
 
 
 def per_device(dlog, dener, energy, mask, owner):
+
+    def apply_cells(packet, link_axis):
+        all_values = jnp.concatenate(
+            lax.all_to_all(
+                jnp.stack([packet for _ in range(lax.psum(1, link_axis))]), link_axis, 0, 0
+            ),
+            axis=1,
+        )
+        return all_values
+
     wdev, width = dlog.shape
     total = wdev * lax.axis_size("walk")
     full = width * lax.axis_size("pan")
@@ -20,7 +30,7 @@
     ocf = om - osum / total
     oc = ocf.astype(jnp.bfloat16)
     hc = ((energy - esum / total)[:, None] * ocf + gm - gsum / total).astype(jnp.bfloat16)
-    gathered = lax.all_gather(oc, "pan", axis=1, tiled=True)
+    gathered = apply_cells(oc, "pan")
     ordered = jnp.take(gathered.reshape(wdev, nblocks, BLOCK), owner, axis=1).reshape(wdev, full)
     right_side = jnp.concatenate([oc, hc], 1)
     dims = (((0,), (0,)), ((), ()))

time: 330 us -> 418 us (1.27)
  waiting for transfers between devices: 200 us -> 289 us
  starting transfers between devices: 0.08 us -> 13.7 us
  local copies, waits for them, and re-layouts: 36.8 us -> 23.2 us
    all_to_all x0 -> x1, waiting for transfers between devices: none -> 183 us  [apply_cells(): lax.all_to_all(jnp.stack([packet for _ in range(lax.psum(1, link_axis))])...]
    all_gather x1 -> x0, waiting for transfers between devices: 89 us -> none  [per_device(): gathered = lax.all_gather(oc, 'pan', axis=1, tiled=True)]
    all_gather x1 -> x0, local copies, waits for them, and re-layouts: 22.6 us -> none  [per_device(): gathered = lax.all_gather(oc, 'pan', axis=1, tiled=True)]
    all_to_all x0 -> x1, starting transfers between devices: none -> 13.7 us  [apply_cells(): lax.all_to_all(jnp.stack([packet for _ in range(lax.psum(1, link_axis))])...]
    another operation x0 -> x1, local copies, waits for them, and re-layouts: none -> 6.01 us  [apply_cells(): jnp.stack([packet for _ in range(lax.psum(1, link_axis))])]
    reduce_scatter x1, waiting for transfers between devices: 111 us -> 105 us  [per_device(): shares = lax.psum_scatter(terms, 'walk', scatter_dimension=0, tiled=True)]
where the time goes in v1:
time: 418 us
  waiting for transfers between devices  289 us (69%)
  blocking collectives  36.5 us (9%)
  local copies, waits for them, and re-layouts  23.2 us (6%)
  matrix products  20.8 us (5%)
  other arithmetic  20.1 us (5%)
  between operations  14.8 us (4%)
  starting transfers between devices  13.7 us (3%)
    all_to_all x1, waiting for transfers between devices, apply_cells(): lax.all_to_all(jnp.stack([packet for _ in range(lax.psum(1, link_axis))])...  183 us
    reduce_scatter x1, waiting for transfers between devices, per_device(): shares = lax.psum_scatter(terms, 'walk', scatter_dimension=0, tiled=True)  105 us
    psum x1, blocking collectives, per_device(): lax.psum((jnp.sum(om, 0), jnp.sum(gm, 0), jnp.sum(energy)), 'walk')  36.5 us
    dot_general x1, matrix products, per_device(): lax.dot_general(ordered, right_side, dims, preferred_element_type=jnp.flo...  20.8 us
    all_to_all x1, starting transfers between devices, apply_cells(): lax.all_to_all(jnp.stack([packet for _ in range(lax.psum(1, link_axis))])...  13.7 us
    gather x1, local copies, waits for them, and re-layouts, per_device(): jnp.take(gathered.reshape(wdev, nblocks, BLOCK), owner, axis=1)  13 us
    select_n x2, other arithmetic, per_device(): jnp.take(gathered.reshape(wdev, nblocks, BLOCK), owner, axis=1)  9.55 us
  transfers between devices with their start and end apart: 2, of which 2 were waited for; matrix products, arithmetic and copies ran while one was open for 0% of the time, Pallas kernels for 0%

profile of v1, /device:TPU:1, one launch (start us, length us, event | category | flops | bytes accessed | tf_op | source)
XLA Modules:
  0.0 418.0 jit_solution(11198472243756360185)
XLA Ops:
  7.2 0.0 copy-start.3
  7.2 0.0 copy-start
  7.2 0.9 dynamic-slice_convert_fusion
  8.1 0.1 broadcast_bitcast_fusion
  8.2 1.3 reduce_sum.28
  9.5 3.1 fusion.4
  12.5 36.5 %all-reduce = (f32[512]{0:T(512)S(1)}, f32[512]{0:T(512)S(1)}, f32[]{:T(128)}) all-reduce(f32[512]{0:T(512)S(1)} %get-tuple-element.3, f32[512]{0:T(512)S(1)} %get-tuple-element.2, f32[]{:T(128)} %reduce_sum.28), channel_id=1, replica_groups=mesh['walk'=16,'pan'=8] {'walk'}, use_global_device_ids=true, to_apply=%region_1.0 | all-reduce | flops 1025 | bytes 8200 | tf_op jit(solution)/shard_map/psum | solution.py:29
  49.7 0.0 copy-done.3
  49.7 0.0 copy-done
  49.7 3.9 subtract_convert_fusion
  53.6 2.9 copy.7
  56.5 6.0 %stack.2 = bf16[8,2048,512]{1,2,0:T(8,128)(2,1)} broadcast(bf16[2048,512]{0,1:T(8,128)(2,1)S(1)} %copy.7), dimensions={1,2} | broadcast | bytes 18874368 | tf_op jit(solution)/shard_map/stack | solution.py:14
  62.5 0.0 copy-start.4
  62.6 13.7 %all-to-all-start = ((bf16[8,2048,512]{1,2,0:T(8,128)(2,1)}), bf16[8,2048,512]{1,2,0:T(8,128)(2,1)}, u32[]{:S(2)}, u32[]{:S(2)}) async-start(bf16[8,2048,512]{1,2,0:T(8,128)(2,1)} %stack.2), calls=%async_computation | async-start | bytes 33554432 | tf_op jit(solution)/shard_map/all_to_all | solution.py:13
  76.2 0.0 reduce-scatter.2.cloned.1.call-start
  76.2 0.0 copy-done.4
  76.2 0.1 broadcast_in_dim.24
  76.3 183.5 %all-to-all-done = bf16[8,2048,512]{1,2,0:T(8,128)(2,1)} async-done(((bf16[8,2048,512]{1,2,0:T(8,128)(2,1)}), bf16[8,2048,512]{1,2,0:T(8,128)(2,1)}, u32[]{:S(2)}, u32[]{:S(2)}) %all-to-all-start) | async-done | bytes 16777248 | tf_op jit(solution)/shard_map/all_to_all | solution.py:13
  259.8 13.0 %gather_fusion = bf16[16,2048,256]{1,2,0:T(8,128)(2,1)} fusion(bf16[2048,16,256]{0,2,1:T(8,128)(2,1)} %bitcast.1, s32[1024]{0:T(1024)S(1)} %pad_clamp_fusion), kind=kCustom, calls=%fused_computation | custom fusion | bytes 33554496 | tf_op jit(solution)/shard_map/jit(_take)/gather | solution.py:34
  272.8 0.0 copy-start.1
  272.9 0.0 copy-start.2
  272.9 9.5 %bitcast_select_fusion = bf16[2048,4096]{0,1:T(8,128)(2,1)S(1)} fusion(bf16[16,2048,256]{1,2,0:T(8,128)(2,1)} %gather_fusion, pred[4096]{0:T(1024)(128)(4,1)S(1)} %broadcast_in_dim.25), kind=kLoop, calls=%fused_computation.1 | loop fusion | flops 8388608 | bytes 33558528 | tf_op jit(solution)/shard_map/jit(_take)/select_n | solution.py:34
  282.4 0.0 copy-done.1
  282.4 0.0 copy-done.2
  282.4 20.8 %fusion = f32[4096,1024]{1,0:T(8,128)} fusion(bf16[2048,4096]{0,1:T(8,128)(2,1)S(1)} %bitcast_select_fusion, bf16[2048,512]{1,0:T(8,128)(2,1)S(1)} %copy-done.2, bf16[2048,512]{1,0:T(8,128)(2,1)S(1)} %copy-done.1), kind=kOutput, calls=%fused_computation.2 | convolution fusion | flops 17188257792 | bytes 37748736 | tf_op jit(solution)/shard_map/dot_general | solution.py:37
  303.3 0.0 reduce-scatter.2.cloned.1.call-update
  303.3 105.4 %reduce-scatter.2.cloned.1.call-done = f32[256,1024]{1,0:T(8,128)} async-done(((f32[4096,1024]{1,0:T(8,128)}), f32[256,1024]{1,0:T(8,128)}) %reduce-scatter.2.cloned.1.call-update) | async-done | bytes 1048592 | tf_op jit(solution)/shard_map/reduce_scatter | solution.py:38
  408.7 1.3 broadcast_multiply_fusion
  410.1 1.0 fusion.9
  (7 shorter events, 0.0 us)
Async XLA Ops:
  7.2 42.5 %copy-start.3 = (f32[2048]{0:T(1024)S(1)}, f32[2048]{0:T(1024)}, u32[]{:S(2)}) copy-start(f32[2048]{0:T(1024)} %param.7) | copy-start | bytes 24580
  7.2 42.5 %copy-start = (bf16[2048,512]{1,0:T(8,128)(2,1)S(1)}, bf16[2048,512]{1,0:T(8,128)(2,1)}, u32[]{:S(2)}) copy-start(bf16[2048,512]{1,0:T(8,128)(2,1)} %param.6) | copy-start | bytes 6291460
  62.5 13.7 %copy-start.4 = (s32[16]{0:T(128)S(1)}, s32[16]{0:T(128)}, u32[]{:S(2)}) copy-start(s32[16]{0:T(128)} %param.9) | copy-start | bytes 196
  62.6 197.3 %all-to-all-start = ((bf16[8,2048,512]{1,2,0:T(8,128)(2,1)}), bf16[8,2048,512]{1,2,0:T(8,128)(2,1)}, u32[]{:S(2)}, u32[]{:S(2)}) async-start(bf16[8,2048,512]{1,2,0:T(8,128)(2,1)} %stack.2), calls=%async_computation | async-start | bytes 33554432 | tf_op jit(solution)/shard_map/all_to_all | solution.py:13
  76.2 332.5 %reduce-scatter.2.cloned.1.call-start = ((), (), s32[]{:S(2)}) async-start(), calls=%async_computation.2 | async-start | bytes 17825792 | tf_op jit(solution)/shard_map/reduce_scatter | solution.py:38
  272.8 9.6 %copy-start.1 = (bf16[2048,512]{1,0:T(8,128)(2,1)S(1)}, bf16[2048,512]{1,0:T(8,128)(2,1)}, u32[]{:S(2)}) copy-start(bf16[2048,512]{1,0:T(8,128)(2,1)} %get-tuple-element.8) | copy-start | bytes 6291460
  272.9 9.6 %copy-start.2 = (bf16[2048,512]{1,0:T(8,128)(2,1)S(1)}, bf16[2048,512]{1,0:T(8,128)(2,1)}, u32[]{:S(2)}) copy-start(bf16[2048,512]{1,0:T(8,128)(2,1)} %get-tuple-element.7) | copy-start | bytes 6291460
Sparse Core Ops, SparseCore 0:
  303.4 105.2 reduce-scatter.1
